TPU v7x, 32 devices: a whole 2x2x4 slice. The times are simulated.
32 devices in a mesh: groups: 2 (over x), depth: 16 (over z, y, core).
Axes of the slice: x: 2, y: 2, z: 4, core: 2. Of those that a mesh axis runs over, the one named last changes fastest.
Arguments:
- voxels: bfloat16 [256, 32, 16384], P(('groups', 'depth')), parts along dimension 0, may hold values from -6 to 6
- offsets: int32 [256], P('groups'), parts along dimension 0, may hold values from 0 to 127
- w_first: bfloat16 [64, 32], replicated, may hold values from -1 to 1
- decoder_second_weight: bfloat16 [33, 64], replicated, may hold values from -0.75 to 0.75
- cotangent: float32 [32, 32768], P(None, ('groups', 'depth')), parts along dimension 1, may hold values from -6 to 6
Outputs:
- image: float32 [32, 32768], P(None, ('groups', 'depth')), parts along dimension 1
- grad_voxels: bfloat16 [256, 32, 16384], P(('groups', 'depth')), parts along dimension 0
- grad_first: float32 [128, 32], P('groups'), parts along dimension 0
- grad_second: float32 [66, 64], P('groups'), parts along dimension 0
There are 2 independent parts, one for each index of `groups`. A program takes and returns all parts, laid end to end along the dimension named above; an argument that names none is the same for every part. Nothing has to cross between parts.
Inputs may be any that keep to these rules, and one draw needn't show every extreme that they name: offsets[p] counts tiles of 128 rays.
All inputs are finite; a program needn't handle non-finite values.
Results may differ from a plain program's by a relative error of at most 0.0085.
Values may be sent and summed in bfloat16 or wider, within the bound.
A program may use at most 192 MiB of HBM per device.

v0:
```python
import functools

import jax
import jax.numpy as jnp
from jax import lax
from jax.experimental import pallas as pl
from jax.experimental.pallas import tpu as pltpu
from jax.sharding import PartitionSpec as P

TILE = 128
PACK = 4
BLOCK = 1024
FSUB = 1024
BSUB = 1024
RELAY = 12
BF = jnp.bfloat16
F32 = jnp.float32
NT = (((1,), (1,)), ((), ()))


def dot(a, b):
    return jnp.dot(a, b, preferred_element_type=F32)


def running_sum(x):
    rows = x.shape[0]
    row = lax.broadcasted_iota(jnp.int32, x.shape, 0)
    s = 1
    while s < rows:
        x = x + jnp.where(row >= s, pltpu.roll(x, s, 0), 0.0)
        s *= 2
    return x


def wrap(t, total):
    if total & (total - 1) == 0:
        return t & (total - 1)
    return lax.rem(t, total)


def first_tile(off_ref, planes, p):
    return off_ref[lax.axis_index("depth") * planes + p]


def tile_at(base, j, rays):
    return pl.ds(pl.multiple_of(wrap(base + j, rays // TILE) * TILE, TILE), TILE)


def shear_kernel(off_ref, vox_ref, x_ref):
    rays = vox_ref.shape[2]
    base = first_tile(off_ref, pl.num_programs(0), pl.program_id(0))
    for j in range(rays // TILE):
        x_ref[:, pl.ds(j * TILE, TILE)] = vox_ref[0, :, tile_at(base, j, rays)]


def shear(offsets, voxels):
    planes, feats, rays = voxels.shape
    return pl.pallas_call(
        shear_kernel,
        grid=(planes,),
        out_shape=jax.ShapeDtypeStruct((planes * feats, rays), BF),
        in_specs=[
            pl.BlockSpec(memory_space=pltpu.SMEM),
            pl.BlockSpec((1, feats, rays), lambda p: (p, 0, 0)),
        ],
        out_specs=pl.BlockSpec((feats, rays), lambda p: (p, 0)),
        name="shear",
    )(offsets, voxels)


def absorb(dens):
    upto = running_sum(dens)
    passing = jnp.exp(-dens)
    before = jnp.exp(dens - upto)
    return upto, passing, before


def softplus(x):
    return jnp.maximum(x, 0.0) + jnp.log1p(jnp.exp(-jnp.abs(x)))


def picks(shape, period, dim):
    other = lax.broadcasted_iota(jnp.int32, shape, 1 - dim)
    return (lax.rem(lax.broadcasted_iota(jnp.int32, shape, dim), period) == other).astype(BF)


def diagonal(shape, rows, cols):
    r = lax.broadcasted_iota(jnp.int32, shape, 0) // rows
    return r == lax.broadcasted_iota(jnp.int32, shape, 1) // cols


def repeat_blocks(w):
    rows, cols = w.shape
    tall = dot(picks((PACK * rows, rows), rows, 0), w).astype(BF)
    full = dot(tall, picks((cols, PACK * cols), cols, 1))
    return jnp.where(diagonal(full.shape, rows, cols), full, 0.0)


def prepare(first_ref, second_ref, w1_ref, w1t_ref, w2_ref, w2t_ref):
    planes = PACK * w2_ref.shape[0]
    chans, hid = second_ref.shape[0] - 1, second_ref.shape[1]
    w1 = repeat_blocks(first_ref[...])
    w1_ref[...] = (0.5 * w1).astype(BF)
    w1t_ref[...] = w1.T.astype(BF)
    rad = repeat_blocks(second_ref[0:chans, :])
    dens = dot(second_ref[chans : chans + 1, :], picks((hid, PACK * hid), hid, 1))
    dens = jnp.broadcast_to(dens, (planes, PACK * hid))
    block = lax.broadcasted_iota(jnp.int32, dens.shape, 1) // hid
    plane = lax.broadcasted_iota(jnp.int32, dens.shape, 0)
    for h in range(planes // PACK):
        mine = jnp.where(plane == block + h * PACK, dens, 0.0)
        w2_ref[h] = jnp.concatenate([0.5 * rad, mine], 0).astype(BF)
        w2t_ref[h] = (0.5 * jnp.concatenate([rad, mine], 0)).T.astype(BF)


def forward_kernel(
    dscale,
    sub,
    x_ref,
    first_ref,
    second_ref,
    cot_ref,
    col_ref,
    cots_ref,
    state_ref,
    w1_ref,
    w1t_ref,
    w2_ref,
    w2t_ref,
    rad_ref,
    cots,
    mine,
    got,
    back,
    land,
    sa,
    ra,
    sb,
    rb,
    s1,
    r1,
    s2,
    r2,
):
    step = pl.program_id(0)
    steps = pl.num_programs(0)
    n = mine.shape[0]
    me = lax.axis_index("depth")
    chip, core = me // 2, lax.rem(me, 2)

    def across_chips(s):
        return pltpu.make_async_remote_copy(
            src_ref=cots.at[chip, core],
            dst_ref=cots.at[chip, core],
            send_sem=sa.at[s],
            recv_sem=ra.at[s],
            device_id={"depth": lax.rem(me + 2 * s, n)},
            device_id_type=pl.DeviceIdType.MESH,
        )

    def to_partner():
        return pltpu.make_async_remote_copy(
            src_ref=cots.at[:, core],
            dst_ref=cots.at[:, core],
            send_sem=sb,
            recv_sem=rb,
            device_id={"depth": me + 1 - 2 * core},
            device_id_type=pl.DeviceIdType.MESH,
        )

    @pl.when(step == 0)
    def _():
        cots[chip, core] = cot_ref[...].astype(BF)
        greet(n, me)
        for s in range(1, n // 2):
            across_chips(s).start()
        prepare(first_ref, second_ref, w1_ref, w1t_ref, w2_ref, w2t_ref)

    @pl.when(step == RELAY * steps // 16)
    def _():
        for s in range(1, n // 2):
            across_chips(s).wait()
        to_partner().start()

    halves, rows = w2_ref.shape[0], w2_ref.shape[1]
    planes = PACK * halves
    per = col_ref.shape[2] // x_ref.shape[1]
    wide = rows - planes
    kin = w1_ref.shape[1]
    chans = col_ref.shape[1]
    for c in range(x_ref.shape[1] // sub):
        here = pl.ds(c * sub, sub)
        raw_d = None
        for h in range(halves):
            half = dot(w1_ref[...], x_ref[pl.ds(h * kin, kin), here])
            hidden = (half + half * jnp.tanh(half)).astype(BF)
            raw = dot(w2_ref[h], hidden)
            rad_ref[pl.ds(h * wide, wide), here] = jnp.tanh(raw[:wide])
            d = raw[wide:]
            raw_d = d if raw_d is None else raw_d + d
        dens = softplus(raw_d) * dscale
        upto, passing, before = absorb(dens)
        weight = 0.5 * before * (1.0 - passing)
        colour = jnp.sum(weight, axis=0, keepdims=True)
        for p in range(planes):
            colour = colour + weight[p : p + 1] * rad_ref[pl.ds(p * chans, chans), here]
        at = pl.multiple_of(lax.rem(step, per) * x_ref.shape[1] + c * sub, TILE)
        col_ref[step // per, :, pl.ds(at, sub)] = colour
        mine[step // per, 0:1, pl.ds(at, sub)] = jnp.exp(-upto[planes - 1 : planes])

    @pl.when(step == steps - 1)
    def _():
        to_partner().wait()
        share_state(n, me, col_ref, cots, cots_ref, state_ref, mine, got, back, land, s1, r1, s2, r2)


def backward_kernel(
    dscale,
    sub,
    off_ref,
    x_ref,
    w1_ref,
    w1t_ref,
    w2_ref,
    w2t_ref,
    cot_ref,
    state_ref,
    gvox_ref,
    acc1_ref,
    acc2_ref,
    slope_ref,
    hid_ref,
    s_ref,
    graw_ref,
    gpre_ref,
):
    step = pl.program_id(0)

    @pl.when(step == 0)
    def _():
        acc1_ref[...] = jnp.zeros_like(acc1_ref)
        acc2_ref[...] = jnp.zeros_like(acc2_ref)

    halves, rows = w2_ref.shape[0], w2_ref.shape[1]
    planes, feats, rays = gvox_ref.shape
    wide = rows - planes
    kin = w1_ref.shape[1]
    kmid = w1_ref.shape[0]
    chans = cot_ref.shape[1]
    width = x_ref.shape[1]
    ones = diagonal((planes, planes * chans), 1, chans).astype(BF)
    for c in range(width // sub):
        here = pl.ds(c * sub, sub)
        cot = cot_ref[0, :, here].astype(F32)
        raw_d = None
        score = 0.5 * jnp.sum(cot, axis=0, keepdims=True)
        for h in range(halves):
            half = dot(w1_ref[...], x_ref[pl.ds(h * kin, kin), here])
            t = jnp.tanh(half)
            up = 1.0 + t
            hidden = half * up
            slope_ref[pl.ds(h * kmid, kmid), here] = up + hidden * (1.0 - t)
            hidden = hidden.astype(BF)
            hid_ref[pl.ds(h * kmid, kmid), here] = hidden
            raw = dot(w2_ref[h], hidden)
            s = jnp.tanh(raw[:wide])
            s_ref[pl.ds(h * wide, wide), here] = s
            prod = jnp.concatenate(
                [(cot * s[k * chans : (k + 1) * chans]).astype(BF) for k in range(PACK)], 0
            )
            score = score + 0.5 * dot(ones[:, h * wide : (h + 1) * wide], prod)
            d = raw[wide:]
            raw_d = d if raw_d is None else raw_d + d
        dens = softplus(raw_d) * dscale
        upto, passing, before = absorb(dens)
        enter = state_ref[0, 0:1, here]
        rest = state_ref[0, 1:2, here]
        before = enter * before
        weight = before * (1.0 - passing)
        running = running_sum(weight * score)
        grad_d = before * passing * score - (rest - running)
        grad_d = (grad_d * (dscale * (0.5 * jnp.tanh(0.5 * raw_d) + 0.5))).astype(BF)
        weight = 0.25 * weight
        for h in range(halves):
            for k in range(PACK):
                p = h * PACK + k
                s = s_ref[pl.ds(p * chans, chans), here]
                graw_ref[h, pl.ds(k * chans, chans), here] = (
                    (weight[p : p + 1] * cot) * (1.0 - s * s)
                ).astype(BF)
            graw_ref[h, pl.ds(wide, planes), here] = grad_d
            ghid = dot(w2t_ref[h], graw_ref[h, :, here])
            gpre = (ghid * slope_ref[pl.ds(h * kmid, kmid), here]).astype(BF)
            gpre_ref[pl.ds(h * kmid, kmid), here] = gpre
            gx = dot(w1t_ref[...], gpre).astype(BF)
            for k in range(PACK):
                p = h * PACK + k
                base = (step * width + c * sub) // TILE + first_tile(off_ref, planes, p)
                for j in range(sub // TILE):
                    gvox_ref[p, :, tile_at(base, j, rays)] = gx[
                        k * feats : (k + 1) * feats, j * TILE : (j + 1) * TILE
                    ]
    for h in range(halves):
        gpre = gpre_ref[pl.ds(h * kmid, kmid), :]
        x = x_ref[pl.ds(h * kin, kin), :]
        hidden = hid_ref[pl.ds(h * kmid, kmid), :]
        acc1_ref[...] += lax.dot_general(gpre, x, NT, preferred_element_type=F32)
        acc2_ref[h] += lax.dot_general(graw_ref[h], hidden, NT, preferred_element_type=F32)


def greet(n, me):
    barrier = pltpu.get_barrier_semaphore()
    for s in range(1, n):
        pl.semaphore_signal(
            barrier,
            inc=1,
            device_id={"depth": lax.rem(me + s, n)},
            device_id_type=pl.DeviceIdType.MESH,
        )
    pl.semaphore_wait(barrier, n - 1)


def swap(n, me, source, target, send_sem, recv_sem):
    copies = []
    for s in range(1, n):
        to = lax.rem(me + s, n)
        copies.append(
            pltpu.make_async_remote_copy(
                src_ref=source(to),
                dst_ref=target.at[me],
                send_sem=send_sem.at[s],
                recv_sem=recv_sem.at[s],
                device_id={"depth": to},
                device_id_type=pl.DeviceIdType.MESH,
            )
        )
    for copy in copies:
        copy.start()
    return copies


def share_state(n, me, col_ref, cots, cots_ref, state_ref, mine, got, back, land, s1, r1, s2, r2):
    def fill(q, carry):
        for core in range(2):
            cot = cots[q, core]
            cots_ref[q, core] = cot
            d = 2 * q + core
            mine[d, 1:2, :] = jnp.sum(col_ref[d] * cot.astype(F32), axis=0, keepdims=True)
        return carry

    lax.fori_loop(0, n // 2, fill, 0)
    copies = swap(n, me, lambda to: mine.at[to], got, s1, r1)
    got[me] = mine[me]
    for copy in copies:
        copy.wait()
    enter = jnp.ones_like(got[0, 0:1, :])
    prior = jnp.zeros_like(enter)
    for d in range(n):
        back[d, 0:1, :] = enter
        back[d, 1:2, :] = prior
        prior = prior + enter * got[d, 1:2, :]
        enter = enter * got[d, 0:1, :]
    for d in range(n):
        back[d, 1:2, :] = prior - back[d, 1:2, :]
    copies = swap(n, me, lambda to: back.at[to], land, s2, r2)
    land[me] = back[me]
    for copy in copies:
        copy.wait()
    state_ref[...] = land[...]


def total_kernel(n, a1_ref, a2_ref, g1_ref, g2_ref, give, got, mine, full, s1, r1, s2, r2):
    me = lax.axis_index("depth")
    greet(n, me)
    hid, feats = g1_ref.shape
    chans = g2_ref.shape[0] - 1
    halves, rows = a2_ref.shape[0], a2_ref.shape[1]
    part = give.shape[1]

    def aligned(ref_rows, k, size):
        at = k * size
        lane = at % TILE
        piece = ref_rows[:, at - lane : at - lane + TILE]
        return pltpu.roll(piece, TILE - lane, 1) if lane else piece

    g1 = g2 = gd = None
    for k in range(PACK):
        one = aligned(a1_ref[pl.ds(k * hid, hid), :], k, feats)
        g1 = one if g1 is None else g1 + one
    for h in range(halves):
        tail = a2_ref[h, pl.ds(PACK * chans, rows - PACK * chans), :]
        row = lax.broadcasted_iota(jnp.int32, (tail.shape[0], TILE), 0)
        for k in range(PACK):
            two = aligned(a2_ref[h, pl.ds(k * chans, chans), :], k, hid)
            g2 = two if g2 is None else g2 + two
            dens = jnp.where(row == h * PACK + k, aligned(tail, k, hid), 0.0)
            dens = jnp.sum(dens, axis=0, keepdims=True)
            gd = dens if gd is None else gd + dens
    lanes = lax.broadcasted_iota(jnp.int32, (hid, TILE), 1)
    rest = hid - chans - 1
    low = jnp.concatenate([g2, gd, jnp.zeros((rest, TILE), F32)], 0)
    both = jnp.where(lanes < hid, low, pltpu.roll(g1, hid, 1))
    for d in range(n):
        give[d] = both[d * part : (d + 1) * part]
    copies = swap(n, me, lambda to: give.at[to], got, s1, r1)
    got[me] = give[me]
    for copy in copies:
        copy.wait()
    mine[...] = jnp.sum(got[...], axis=0)
    copies = swap(n, me, lambda to: mine, full, s2, r2)
    full[me] = mine[...]
    for copy in copies:
        copy.wait()
    both = jnp.concatenate([full[d] for d in range(n)], 0)
    g2_ref[...] = both[: chans + 1, :hid]
    g1_ref[...] = pltpu.roll(both, TILE - hid, 1)[:, :feats]


def total_over_depth(n, acc1, acc2, first, second):
    vmem = pl.BlockSpec(memory_space=pltpu.VMEM)
    part = (n, first[0] // n, TILE)
    return pl.pallas_call(
        functools.partial(total_kernel, n),
        out_shape=(jax.ShapeDtypeStruct(first, F32), jax.ShapeDtypeStruct(second, F32)),
        in_specs=[vmem] * 2,
        out_specs=(vmem, vmem),
        scratch_shapes=[
            pltpu.VMEM(part, F32),
            pltpu.VMEM(part, F32),
            pltpu.VMEM(part[1:], F32),
            pltpu.VMEM(part, F32),
        ]
        + [pltpu.SemaphoreType.DMA((n,))] * 4,
        compiler_params=pltpu.CompilerParams(collective_id=2, has_side_effects=True),
        name="total_over_depth",
    )(acc1, acc2)


def shards(voxels, offsets, w_first, w_second, cotangent):
    planes, feats, rays = voxels.shape
    hid = w_first.shape[0]
    chans, chunk = cotangent.shape
    n = lax.axis_size("depth")
    halves = planes // PACK
    dscale = 3.0 / (planes * n)
    block = min(BLOCK, chunk)
    per = chunk // block
    steps = rays // block

    smem = pl.BlockSpec(memory_space=pltpu.SMEM)
    vmem = pl.BlockSpec(memory_space=pltpu.VMEM)

    def ray_spec(rows):
        return pl.BlockSpec((1, rows, block), lambda i: (i // per, 0, i % per))

    params = pltpu.CompilerParams(vmem_limit_bytes=60 * 2**20)
    rows = PACK * chans + planes
    weights = (
        jax.ShapeDtypeStruct((PACK * hid, PACK * feats), BF),
        jax.ShapeDtypeStruct((PACK * feats, PACK * hid), BF),
        jax.ShapeDtypeStruct((halves, rows, PACK * hid), BF),
        jax.ShapeDtypeStruct((halves, PACK * hid, rows), BF),
    )
    x_spec = pl.BlockSpec((planes * feats, block), lambda i: (0, i))
    sheared = shear(offsets, voxels)
    halved = (n // 2, 2, chans, chunk)
    pair = (n, 2, chunk)
    colour, cot, state, *weights = pl.pallas_call(
        functools.partial(forward_kernel, dscale, min(FSUB, block)),
        grid=(steps,),
        out_shape=(
            jax.ShapeDtypeStruct((n, chans, chunk), F32),
            jax.ShapeDtypeStruct(halved, BF),
            jax.ShapeDtypeStruct(pair, F32),
        )
        + weights,
        in_specs=[x_spec] + [vmem] * 3,
        out_specs=(vmem,) * 7,
        scratch_shapes=[
            pltpu.VMEM((planes * chans, block), F32),
            pltpu.VMEM(halved, BF),
        ]
        + [pltpu.VMEM(pair, F32)] * 4
        + [pltpu.SemaphoreType.DMA((n // 2,))] * 2
        + [pltpu.SemaphoreType.DMA] * 2
        + [pltpu.SemaphoreType.DMA((n,))] * 4,
        compiler_params=pltpu.CompilerParams(
            vmem_limit_bytes=60 * 2**20, collective_id=1, has_side_effects=True
        ),
        cost_estimate=pl.CostEstimate(
            flops=8 * 10**9, bytes_accessed=12 * 2**20, transcendentals=10**7
        ),
        name="forward",
    )(sheared, w_first, w_second, cotangent)
    cot = cot.reshape(n, chans, chunk)
    share = (state[:, 0:1, :] * colour).astype(BF)
    image = lax.psum_scatter(share, "depth", scatter_dimension=0).astype(F32)
    gvox, acc1, acc2 = pl.pallas_call(
        functools.partial(backward_kernel, dscale, min(BSUB, block)),
        grid=(steps,),
        out_shape=(
            jax.ShapeDtypeStruct(voxels.shape, BF),
            jax.ShapeDtypeStruct((PACK * hid, PACK * feats), F32),
            jax.ShapeDtypeStruct((halves, rows, PACK * hid), F32),
        ),
        in_specs=[smem, x_spec] + [vmem] * 4 + [ray_spec(chans), ray_spec(2)],
        out_specs=(vmem, vmem, vmem),
        scratch_shapes=[
            pltpu.VMEM((planes * hid, block), F32),
            pltpu.VMEM((planes * hid, block), BF),
            pltpu.VMEM((planes * chans, block), F32),
            pltpu.VMEM((halves, rows, block), BF),
            pltpu.VMEM((planes * hid, block), BF),
        ],
        compiler_params=params,
        cost_estimate=pl.CostEstimate(
            flops=60 * 10**9, bytes_accessed=24 * 2**20, transcendentals=10**7
        ),
        name="backward",
    )(offsets, sheared, *weights, cot, state)
    grad_first, grad_second = total_over_depth(n, acc1, acc2, w_first.shape, w_second.shape)
    return image, gvox, grad_first, grad_second


def solution(mesh):
    placed = (
        P(("groups", "depth"), None, None),
        P("groups"),
        P(),
        P(),
        P(None, ("groups", "depth")),
    )
    return jax.shard_map(
        shards,
        mesh=mesh,
        in_specs=placed,
        out_specs=(
            P(None, ("groups", "depth")),
            P(("groups", "depth"), None, None),
            P("groups", None),
            P("groups", None),
        ),
        check_vma=False,
    )
```

profile of v0, /device:TPU:0, one launch (start us, length us, event | category | flops | bytes accessed | tf_op | source)
XLA Modules:
  0.0 130.1 jit_solution(5585575174043918838)
XLA Ops:
  7.2 0.0 reduce-scatter.2.cloned.1.call-start
  7.2 1.4 %copy.9.first_ref = bf16[64,32]{1,0:T(8,128)(2,1)} copy(bf16[64,32]{0,1:T(8,128)(2,1)} %param.7) | data formatting | bytes 8192 | tf_op args[2]
  8.6 9.8 %shear.1.x_ref = bf16[256,16384]{1,0:T(8,128)(2,1)} custom-call(s32[128]{0:T(128)} %off_ref.3, bf16[8,32,16384]{2,1,0:T(8,128)(2,1)} %vox_ref.1), custom_call_target="tpu_custom_call" | custom-call | tf_op jit(solution)/shard_map/shear/pallas_call | solution.py:58
  18.4 36.7 %forward.1 = (f32[16,32,1024]{2,1,0:T(8,128)}, bf16[8,2,32,1024]{3,2,1,0:T(8,128)(2,1)}, f32[16,2,1024]{2,1,0:T(2,128)}, bf16[256,128]{1,0:T(8,128)(2,1)}, bf16[...) custom-call(bf16[256,16384]{1,0:T(8,128)(2,1)} %shear.1.x_ref, ...), custom_call_target="tpu_custom_call" | custom-call | flops 8000000000 | bytes 12582912 | tf_op jit(solution)/shard_map/forward/pallas_call | solution.py:468
  55.1 1.0 slice.3
  56.1 2.9 %multiply_convert_fusion = bf16[16,32,1024]{2,1,0:T(8,128)(2,1)} fusion(f32[16,32,1024]{2,1,0:T(8,128)} %get-tuple-element.17, f32[16,1024]{1,0:T(8,128)S(1)} %bitcast.7), kind=kLoop, calls=%fused_computation | loop fusion | flops 1048576 | bytes 3211264 | tf_op jit(solution)/shard_map/convert_element_type | solution.py:496
  58.9 0.0 reduce-scatter.2.cloned.1.call-update
  59.0 46.3 %backward.1 = (bf16[8,32,16384]{2,1,0:T(8,128)(2,1)}, f32[256,128]{1,0:T(8,128)}, f32[2,136,256]{2,1,0:T(8,128)}) custom-call(s32[128]{0:T(128)} %off_ref.3, bf16[256,16384]{1,0:T(8,128)(2,1)} %shear.1.x_ref, bf16[256,128]{1,0:T(8,128)(2,1)} %get-tuple-element.18.w1_ref, bf16[128,256]{1,0:T(8,128)(2,1)} %get-tuple-element.19.w1t_ref, ...), custom_call_target="tpu_custom_call" | custom-call | flops 60000002048 | bytes 25165824 | tf_op jit(solution)/shard_map/backward/pallas_call | solution.py:498
  105.3 13.7 %total_over_depth.1 = (f32[64,32]{1,0:T(8,128)}, f32[33,64]{1,0:T(8,128)}) custom-call(f32[256,128]{1,0:T(8,128)} %get-tuple-element.24.a1_ref, f32[2,136,256]{2,1,0:T(8,128)} %get-tuple-element.25.a2_ref), custom_call_target="tpu_custom_call" | custom-call | tf_op jit(solution)/shard_map/total_over_depth/pallas_call | solution.py:422
  119.0 1.4 %copy.10 = f32[64,32]{0,1:T(8,128)} copy(f32[64,32]{1,0:T(8,128)} %get-tuple-element.30) | data formatting | bytes 16384
  120.4 0.0 reduce-scatter.2.cloned.1.call-done
  120.4 1.5 %bitcast_convert_fusion = f32[32,1024]{1,0:T(8,128)} fusion(bf16[1,32,1024]{2,1,0:T(8,128)(2,1)} %reduce-scatter.2.cloned.1.call-done), kind=kLoop, calls=%fused_computation.2 | loop fusion | flops 32768 | bytes 196608 | tf_op jit(solution)/shard_map/convert_element_type | solution.py:497
  121.9 1.3 %copy.15 = f32[33,64]{1,0:T(8,128)} copy(f32[33,64]{1,0:T(8,128)} %get-tuple-element.39) | data formatting | bytes 16896
  (1 shorter events, 0.0 us)
Async XLA Ops:
  7.2 113.2 %reduce-scatter.2.cloned.1.call-start = ((), (), s32[]{:S(2)}) async-start(), calls=%async_computation.1 | async-start | bytes 1114112 | tf_op jit(solution)/shard_map/reduce_scatter | solution.py:497
Sparse Core Ops, SparseCore 0:
  59.1 57.5 reduce-scatter.1
where the time goes:
time: 131 us; the launch traced here: 130 us
  Pallas kernels  106 us (81%)
  between operations  14.1 us (11%)
  local copies, waits for them, and re-layouts  5.12 us (4%)
  other arithmetic  4.37 us (3%)
    pallas_call x1, Pallas kernels, shards(): pl.pallas_call(functools.partial(backward_kernel, dscale, min(BSUB, block...  46.3 us
    pallas_call x1, Pallas kernels, shards(): pl.pallas_call(functools.partial(forward_kernel, dscale, min(FSUB, block)...  36.7 us
    pallas_call x1, Pallas kernels, total_over_depth(): pl.pallas_call(functools.partial(total_kernel, n), out_shape=(jax.ShapeDt...  13.7 us
    pallas_call x1, Pallas kernels, shear(): pl.pallas_call(shear_kernel, grid=(planes,), out_shape=jax.ShapeDtypeStru...  9.76 us
    unnamed x4, local copies, waits for them, and re-layouts  4.17 us
    convert_element_type x1, other arithmetic, shards(): share = (state[:, 0:1, :] * colour).astype(BF)  2.87 us
  transfers between devices with their start and end apart: 1, of which 0 were waited for; matrix products, arithmetic and copies ran while one was open for 1% of the time, Pallas kernels for 46%

commit v1 on v0

v1 whole, which is shorter than its diff:
```python
import functools

import jax
import jax.numpy as jnp
from jax import lax
from jax.experimental import pallas as pl
from jax.experimental.pallas import tpu as pltpu
from jax.sharding import PartitionSpec as P

TILE = 128
PACK = 4
FSUB = 256
BSUB = 256
GSUB = 512
LIMIT = 191 * 2**18
BF = jnp.bfloat16
F32 = jnp.float32
NT = (((1,), (1,)), ((), ()))


def dot(a, b):
    return jnp.dot(a, b, preferred_element_type=F32)


def running_sum(x):
    rows = x.shape[0]
    row = lax.broadcasted_iota(jnp.int32, x.shape, 0)
    s = 1
    while s < rows:
        x = x + jnp.where(row >= s, pltpu.roll(x, s, 0), 0.0)
        s *= 2
    return x


def wrap(t, total):
    if total & (total - 1) == 0:
        return t & (total - 1)
    return lax.rem(t, total)


def first_tile(off_ref, planes, p):
    return off_ref[lax.axis_index("depth") * planes + p]


def tile_at(base, j, rays):
    return pl.ds(pl.multiple_of(wrap(base + j, rays // TILE) * TILE, TILE), TILE)


def absorb(dens):
    upto = running_sum(dens)
    passing = jnp.exp(-dens)
    before = jnp.exp(dens - upto)
    return upto, passing, before


def softplus(x):
    return jnp.maximum(x, 0.0) + jnp.log1p(jnp.exp(-jnp.abs(x)))


def picks(shape, period, dim):
    other = lax.broadcasted_iota(jnp.int32, shape, 1 - dim)
    return (lax.rem(lax.broadcasted_iota(jnp.int32, shape, dim), period) == other).astype(BF)


def diagonal(shape, rows, cols):
    r = lax.broadcasted_iota(jnp.int32, shape, 0) // rows
    return r == lax.broadcasted_iota(jnp.int32, shape, 1) // cols


def repeat_blocks(w):
    rows, cols = w.shape
    tall = dot(picks((PACK * rows, rows), rows, 0), w).astype(BF)
    full = dot(tall, picks((cols, PACK * cols), cols, 1))
    return jnp.where(diagonal(full.shape, rows, cols), full, 0.0)


def prepare(first_ref, second_ref, w1_ref, w1t_ref, w2_ref, w2t_ref):
    planes = PACK * w2_ref.shape[0]
    chans, hid = second_ref.shape[0] - 1, second_ref.shape[1]
    w1t = repeat_blocks(first_ref[...])
    w1t_ref[...] = w1t.astype(BF)
    w1_ref[...] = (0.5 * w1t).T.astype(BF)
    rad = repeat_blocks(second_ref[0:chans, :])
    dens = dot(second_ref[chans : chans + 1, :], picks((hid, PACK * hid), hid, 1))
    dens = jnp.broadcast_to(dens, (planes, PACK * hid))
    block = lax.broadcasted_iota(jnp.int32, dens.shape, 1) // hid
    plane = lax.broadcasted_iota(jnp.int32, dens.shape, 0)
    for h in range(planes // PACK):
        mine = jnp.where(plane == block + h * PACK, dens, 0.0)
        w2_ref[h] = jnp.concatenate([0.5 * rad, mine], 0).astype(BF)
        w2t_ref[h] = (0.5 * jnp.concatenate([rad, mine], 0)).T.astype(BF)


def remote(src, dst, send_sem, recv_sem, to):
    return pltpu.make_async_remote_copy(
        src_ref=src,
        dst_ref=dst,
        send_sem=send_sem,
        recv_sem=recv_sem,
        device_id={"depth": to},
        device_id_type=pl.DeviceIdType.MESH,
    )


def turn(i, n):
    if n & (n - 1):
        return i
    c, bit = 0, 1
    while bit < n:
        c = c + ((i // bit) % 2) * (n // (2 * bit))
        bit *= 2
    return c


def each(n, body):
    def step(d, carry):
        body(d)
        return carry

    lax.fori_loop(0, n, step, 0)


def fused_kernel(
    dscale,
    xs,
    first_ref,
    second_ref,
    cot_ref,
    image_ref,
    gsh,
    g1_ref,
    g2_ref,
    hids,
    slope,
    srad,
    wgt,
    bpass,
    dsig,
    graw,
    w1,
    w1t,
    w2,
    w2t,
    acc1,
    acc2,
    cots,
    csend,
    crecv,
    tsend,
    trecv,
    back,
    land,
    held,
    give,
    got,
    mine,
    full,
    sem_c,
    rem_c,
    sem_t,
    rem_t,
    sem_b,
    rem_b,
    sem_k,
    rem_k,
    sem_r,
    s1,
    r1,
    s2,
    r2,
):
    n, chans, width = cots.shape
    halves, rows = w2.shape[0], w2.shape[1]
    planes = PACK * halves
    feats = xs.shape[1] // planes
    kin, kmid = w1.shape[1], w1.shape[0]
    wide = rows - planes
    lag = n // 2
    me = lax.axis_index("depth")
    chip, core = me // 2, me % 2
    partner = me + 1 - 2 * core

    barrier = pltpu.get_barrier_semaphore()
    for s in range(1, n):
        pl.semaphore_signal(
            barrier,
            inc=1,
            device_id={"depth": (me + s) % n},
            device_id_type=pl.DeviceIdType.MESH,
        )
    cots[me] = cot_ref[...].astype(BF)
    acc1[...] = jnp.zeros_like(acc1)
    acc2[...] = jnp.zeros_like(acc2)
    prepare(first_ref, second_ref, w1, w1t, w2, w2t)
    pl.semaphore_wait(barrier, n - 1)

    def colour_copy(c):
        return remote(csend.at[c], crecv.at[me], sem_c.at[c], rem_c.at[me], c)

    def colour_here(d):
        return remote(csend.at[d], crecv.at[d], sem_c.at[d], rem_c.at[d], d)

    def through_copy(c):
        return remote(tsend.at[c], trecv.at[me], sem_t.at[c], rem_t.at[me], c)

    def through_here(d):
        return remote(tsend.at[d], trecv.at[d], sem_t.at[d], rem_t.at[d], d)

    def reply_copy(d):
        return remote(back.at[d], land.at[me], sem_b.at[d], rem_b.at[me], d)

    def reply_here(c):
        return remote(back.at[c], land.at[c], sem_b.at[c], rem_b.at[c], c)

    def cot_copy(s):
        to = partner if s == 0 else (me + 2 * s) % n
        return remote(cots.at[me], cots.at[me], sem_k.at[s], rem_k.at[me], to)

    def relay_copy(c):
        return remote(cots.at[c], cots.at[c], sem_r.at[c], rem_k.at[c], partner)

    def hand_on(c):
        @pl.when(c != me)
        def _():
            colour_copy(c).start()
            through_copy(c).start()

        @pl.when(c == me)
        def _():
            crecv[me] = csend[me]
            trecv[me] = tsend[me]

    def relays(c):
        return jnp.logical_and(c % 2 == core, c != me)

    def settle():
        def arrived(d):
            @pl.when(d != me)
            def _():
                colour_here(d).wait_recv()
                through_here(d).wait_recv()

        each(n, arrived)
        cot = cot_ref[...]

        row = lax.broadcasted_iota(jnp.int32, held.shape, 0)
        held[...] = (row == 0).astype(F32)
        image_ref[...] = jnp.zeros_like(image_ref)

        def fold(d):
            enter = held[0:1, :]
            prior = held[1:2, :]
            colour = crecv[d].astype(F32)
            back[d, 0:1, :] = enter
            back[d, 1:2, :] = prior
            held[2:3, :] = trecv[d]
            image_ref[...] += enter * colour
            held[1:2, :] = prior + enter * jnp.sum(cot * colour, axis=0, keepdims=True)
            held[0:1, :] = enter * held[2:3, :]

        each(n, fold)
        total = held[1:2, :]

        def turn_round(d):
            back[d, 1:2, :] = total - back[d, 1:2, :]

        each(n, turn_round)

        def answer(d):
            @pl.when(d != me)
            def _():
                reply_copy(d).start()

        each(n, answer)
        land[me] = back[me]

    def later(c):
        @pl.when(relays(c))
        def _():
            relay_copy(c).wait_recv()
            relay_copy(c).start()

        @pl.when(c == me)
        def _():
            settle()

    fsub = min(FSUB, width)

    def forward(i, carry):
        c = turn(i, n)

        @pl.when(i > 0)
        def _():
            hand_on(turn(i - 1, n))

        @pl.when(c == me)
        def _():
            for s in range(n // 2):
                cot_copy(s).start()

        @pl.when(i >= lag)
        def _():
            later(turn(i - lag, n))

        for b in range(width // fsub):
            here = pl.ds(b * fsub, fsub)
            raw_d = None
            for h in range(halves):
                x = xs[c, pl.ds(h * kin, kin), here]
                half = dot(w1[...], x)
                t = jnp.tanh(half)
                up = 1.0 + t
                hidden = half * up
                slope[c, pl.ds(h * kmid, kmid), here] = (up + hidden * (1.0 - t)).astype(BF)
                hidden = hidden.astype(BF)
                hids[c, pl.ds(h * kmid, kmid), here] = hidden
                out = dot(w2[h], hidden)
                srad[c, pl.ds(h * wide, wide), here] = jnp.tanh(out[:wide]).astype(BF)
                d = out[wide:]
                raw_d = d if raw_d is None else raw_d + d
            dens = softplus(raw_d) * dscale
            upto, passing, before = absorb(dens)
            weight = before * (1.0 - passing)
            wgt[c, :, here] = weight
            bpass[c, :, here] = before * passing
            dsig[c, :, here] = dscale * (0.5 * jnp.tanh(0.5 * raw_d) + 0.5)
            weight = 0.5 * weight
            colour = jnp.sum(weight, axis=0, keepdims=True)
            for p in range(planes):
                s = srad[c, pl.ds(p * chans, chans), here].astype(F32)
                colour = colour + weight[p : p + 1] * s
            csend[c, :, here] = colour.astype(BF)
            tsend[c, :, here] = jnp.exp(-upto[planes - 1 : planes])
        return carry

    lax.fori_loop(0, n, forward, 0)

    ones = diagonal((planes, planes * chans), 1, chans).astype(BF)
    bsub = min(BSUB, width)

    def backward(i, carry):
        c = turn(i, n)

        @pl.when(i == 0)
        def _():
            hand_on(turn(n - 1, n))

        @pl.when(i < n - lag)
        def _():
            later(turn(i + lag, n))

        @pl.when(c % 2 != core)
        def _():
            relay_copy(c).wait_recv()

        @pl.when(c != me)
        def _():
            reply_here(c).wait_recv()

        for b in range(width // bsub):
            here = pl.ds(b * bsub, bsub)
            cot = cots[c, :, here]
            prod = jnp.concatenate(
                [cot * srad[c, pl.ds(p * chans, chans), here] for p in range(planes)], 0
            )
            score = 0.5 * (jnp.sum(cot.astype(F32), axis=0, keepdims=True) + dot(ones, prod))
            enter = land[c, 0:1, here]
            rest = land[c, 1:2, here]
            weight = enter * wgt[c, :, here]
            running = running_sum(weight * score)
            grad_d = enter * bpass[c, :, here] * score - (rest - running)
            grad_d = (grad_d * dsig[c, :, here]).astype(BF)
            weight = 0.25 * weight
            for h in range(halves):
                for k in range(PACK):
                    p = h * PACK + k
                    s = srad[c, pl.ds(p * chans, chans), here]
                    w = jnp.broadcast_to(weight[p : p + 1], (chans, bsub)).astype(BF)
                    graw[h, pl.ds(k * chans, chans), here] = (w * cot) * (1.0 - s * s)
                graw[h, pl.ds(wide, planes), here] = grad_d
                ghid = dot(w2t[h], graw[h, :, here]).astype(BF)
                mid = pl.ds(h * kmid, kmid)
                slope[c, mid, here] = ghid * slope[c, mid, here]
        for h in range(halves):
            mid = pl.ds(h * kmid, kmid)
            acc1[...] += lax.dot_general(
                slope[c, mid, :], xs[c, pl.ds(h * kin, kin), :], NT, preferred_element_type=F32
            )
            acc2[h] += lax.dot_general(graw[h], hids[c, mid, :], NT, preferred_element_type=F32)
        return carry

    lax.fori_loop(0, n, backward, 0)

    fold_grads(n, acc1, acc2, feats, chans, give)
    copies = swap(n, me, lambda to: give.at[to], got, s1, r1)
    got[me] = give[me]

    gsub = min(GSUB, width)

    def voxel_grads(c, carry):
        for b in range(width // gsub):
            here = pl.ds(b * gsub, gsub)
            for h in range(halves):
                gx = dot(w1t[...], slope[c, pl.ds(h * kmid, kmid), here])
                gsh[c, pl.ds(h * kin, kin), here] = gx.astype(BF)
        return carry

    lax.fori_loop(0, n // 2, voxel_grads, 0)
    for copy in copies:
        copy.wait()
    mine[...] = jnp.sum(got[...], axis=0)
    copies = swap(n, me, lambda to: mine, full, s2, r2)
    full[me] = mine[...]
    lax.fori_loop(n // 2, n, voxel_grads, 0)
    for copy in copies:
        copy.wait()
    both = jnp.concatenate([full[d] for d in range(n)], 0)
    g2_ref[...] = both[: chans + 1, : both.shape[0]]
    square = jnp.concatenate([both, jnp.zeros_like(both)], 0).T
    g1_ref[...] = square[both.shape[0] : both.shape[0] + feats, : both.shape[0]]

    def finish(d):
        @pl.when(d != me)
        def _():
            colour_copy(d).wait_send()
            through_copy(d).wait_send()
            reply_copy(d).wait_send()

        @pl.when(relays(d))
        def _():
            relay_copy(d).wait_send()

    each(n, finish)
    for s in range(n // 2):
        cot_copy(s).wait_send()


def swap(n, me, source, target, send_sem, recv_sem):
    copies = []
    for s in range(1, n):
        to = lax.rem(me + s, n)
        copies.append(remote(source(to), target.at[me], send_sem.at[s], recv_sem.at[s], to))
    for copy in copies:
        copy.start()
    return copies


def fold_grads(n, a1_ref, a2_ref, feats, chans, give):
    hid = a1_ref.shape[0] // PACK
    halves, rows = a2_ref.shape[0], a2_ref.shape[1]
    part = give.shape[1]

    def aligned(ref_rows, k, size):
        at = k * size
        lane = at % TILE
        piece = ref_rows[:, at - lane : at - lane + TILE]
        return pltpu.roll(piece, TILE - lane, 1) if lane else piece

    g1 = g2 = gd = None
    for k in range(PACK):
        one = aligned(a1_ref[pl.ds(k * hid, hid), :], k, feats)
        g1 = one if g1 is None else g1 + one
    for h in range(halves):
        tail = a2_ref[h, pl.ds(PACK * chans, rows - PACK * chans), :]
        row = lax.broadcasted_iota(jnp.int32, (tail.shape[0], TILE), 0)
        for k in range(PACK):
            two = aligned(a2_ref[h, pl.ds(k * chans, chans), :], k, hid)
            g2 = two if g2 is None else g2 + two
            dens = jnp.where(row == h * PACK + k, aligned(tail, k, hid), 0.0)
            dens = jnp.sum(dens, axis=0, keepdims=True)
            gd = dens if gd is None else gd + dens
    lanes = lax.broadcasted_iota(jnp.int32, (hid, TILE), 1)
    rest = hid - chans - 1
    low = jnp.concatenate([g2, gd, jnp.zeros((rest, TILE), F32)], 0)
    both = jnp.where(lanes < hid, low, pltpu.roll(g1, hid, 1))
    for d in range(n):
        give[d] = both[d * part : (d + 1) * part]


def moves(off_ref, planes, feats, n, width, rays, pair):
    me = lax.axis_index("depth")
    tiles, per = rays // TILE, width // TILE
    for p in range(planes):
        base = off_ref[me * planes + p]
        rows = pl.ds(p * feats, feats)

        def chunk(c):
            first = wrap(base + c * per, tiles)

            @pl.when(first + per <= tiles)
            def _():
                at = pl.ds(pl.multiple_of(first * TILE, TILE), width)
                pair((p, slice(None), at), (c, rows)).start()

            @pl.when(first + per > tiles)
            def _():
                for j in range(per):
                    spot = (c, rows, pl.ds(j * TILE, TILE))
                    pair((p, slice(None), tile_at(first, j, rays)), spot).start()

        each(n, chunk)


def shear_kernel(off_ref, vox_ref, x_ref, sem):
    planes, feats, rays = vox_ref.shape
    n, _, width = x_ref.shape

    def pair(plain, sheared):
        return pltpu.make_async_copy(vox_ref.at[plain], x_ref.at[sheared], sem)

    moves(off_ref, planes, feats, n, width, rays, pair)
    pltpu.make_async_copy(x_ref, x_ref, sem).wait()


def place_kernel(off_ref, gsh_ref, image_in, g1_in, g2_in, gvox_ref, image_ref, g1_ref, g2_ref, sem):
    planes, feats, rays = gvox_ref.shape
    n, _, width = gsh_ref.shape

    def pair(plain, sheared):
        return pltpu.make_async_copy(gsh_ref.at[sheared], gvox_ref.at[plain], sem)

    moves(off_ref, planes, feats, n, width, rays, pair)
    image_ref[...] = image_in[...]
    g1_ref[...] = g1_in[...]
    g2_ref[...] = g2_in[...]
    pltpu.make_async_copy(gsh_ref, gsh_ref, sem).wait()


def shards(voxels, offsets, w_first, w_second, cotangent):
    planes, feats, rays = voxels.shape
    hid = w_first.shape[0]
    chans, chunk = cotangent.shape
    n = lax.axis_size("depth")
    halves = planes // PACK
    dscale = 3.0 / (planes * n)
    rows = PACK * chans + planes

    smem = pl.BlockSpec(memory_space=pltpu.SMEM)
    vmem = pl.BlockSpec(memory_space=pltpu.VMEM)
    hbm = pl.BlockSpec(memory_space=pltpu.HBM)
    small = (
        jax.ShapeDtypeStruct((chans, chunk), F32),
        jax.ShapeDtypeStruct((feats, hid), F32),
        jax.ShapeDtypeStruct((chans + 1, hid), F32),
    )
    part = (n, hid // n, TILE)
    dma = pltpu.SemaphoreType.DMA
    chunks = pltpu.VMEM((n, planes * feats, chunk), BF)
    sheared = pl.pallas_call(
        shear_kernel,
        out_shape=chunks,
        in_specs=[smem, hbm],
        out_specs=vmem,
        scratch_shapes=[dma],
        compiler_params=pltpu.CompilerParams(vmem_limit_bytes=4 * 2**20),
        name="shear",
    )(offsets, pltpu.with_memory_space_constraint(voxels, pltpu.HBM))
    image, gsh, g1, g2 = pl.pallas_call(
        functools.partial(fused_kernel, dscale),
        out_shape=(small[0], chunks) + small[1:],
        in_specs=[vmem, vmem, vmem, vmem],
        out_specs=(vmem, vmem, vmem, vmem),
        scratch_shapes=[
            pltpu.VMEM((n, planes * hid, chunk), BF),
            pltpu.VMEM((n, planes * hid, chunk), BF),
            pltpu.VMEM((n, planes * chans, chunk), BF),
            pltpu.VMEM((n, planes, chunk), F32),
            pltpu.VMEM((n, planes, chunk), F32),
            pltpu.VMEM((n, planes, chunk), F32),
            pltpu.VMEM((halves, rows, chunk), BF),
            pltpu.VMEM((PACK * hid, PACK * feats), BF),
            pltpu.VMEM((PACK * feats, PACK * hid), BF),
            pltpu.VMEM((halves, rows, PACK * hid), BF),
            pltpu.VMEM((halves, PACK * hid, rows), BF),
            pltpu.VMEM((PACK * hid, PACK * feats), F32),
            pltpu.VMEM((halves, rows, PACK * hid), F32),
            pltpu.VMEM((n, chans, chunk), BF),
            pltpu.VMEM((n, chans, chunk), BF),
            pltpu.VMEM((n, chans, chunk), BF),
            pltpu.VMEM((n, 1, chunk), F32),
            pltpu.VMEM((n, 1, chunk), F32),
            pltpu.VMEM((n, 2, chunk), F32),
            pltpu.VMEM((n, 2, chunk), F32),
            pltpu.VMEM((8, chunk), F32),
            pltpu.VMEM(part, F32),
            pltpu.VMEM(part, F32),
            pltpu.VMEM(part[1:], F32),
            pltpu.VMEM(part, F32),
        ]
        + [dma((n,))] * 6
        + [dma((n // 2,)), dma((n,)), dma((n,))]
        + [dma((n,))] * 4,
        compiler_params=pltpu.CompilerParams(
            vmem_limit_bytes=LIMIT, collective_id=1, has_side_effects=True
        ),
        name="fused",
    )(pltpu.with_memory_space_constraint(sheared, pltpu.VMEM), w_first.T, w_second, cotangent)
    gvox, image, g1, g2 = pl.pallas_call(
        place_kernel,
        out_shape=(jax.ShapeDtypeStruct(voxels.shape, BF),) + small,
        in_specs=[smem] + [vmem] * 4,
        out_specs=(hbm, vmem, vmem, vmem),
        scratch_shapes=[dma],
        compiler_params=pltpu.CompilerParams(vmem_limit_bytes=4 * 2**20),
        name="place",
    )(offsets, pltpu.with_memory_space_constraint(gsh, pltpu.VMEM), image, g1, g2)
    return image, gvox, g1.T, g2


def solution(mesh):
    placed = (
        P(("groups", "depth"), None, None),
        P("groups"),
        P(),
        P(),
        P(None, ("groups", "depth")),
    )
    return jax.shard_map(
        shards,
        mesh=mesh,
        in_specs=placed,
        out_specs=(
            P(None, ("groups", "depth")),
            P(("groups", "depth"), None, None),
            P("groups", None),
            P("groups", None),
        ),
        check_vma=False,
    )
```

time: 131 us -> 98.3 us (0.75)
  between operations: 14.1 us -> 0.68 us
  Pallas kernels: 106 us -> 94.2 us
  other arithmetic: 4.37 us -> 0 us
  local copies, waits for them, and re-layouts: 5.12 us -> 3 us
    pallas_call x4 -> x3, Pallas kernels: 106 us -> 94.2 us  [the longest x1 83.3 us: shards(): pl.pallas_call(functools.partial(fused_kernel, dscale), out_shape=(small[...]
    convert_element_type x2 -> x0, other arithmetic: 4.37 us -> none  [the longest x1 2.87 us: shards(): share = (state[:, 0:1, :] * colour).astype(BF)]
    unnamed x4 -> x10, local copies, waits for them, and re-layouts: 4.17 us -> 3 us
  transfers between devices with their start and end apart: 1 -> 0, of which waited for: 0 -> 0; matrix products, arithmetic and copies ran while one was open for 1% -> 0% of each run, Pallas kernels for 46% -> 0%
where the time goes in v1:
time: 98.3 us; the launch traced here: 97.9 us
  Pallas kernels  94.2 us (96%)
  local copies, waits for them, and re-layouts  3 us (3%)
    pallas_call x1, Pallas kernels, shards(): pl.pallas_call(functools.partial(fused_kernel, dscale), out_shape=(small[...  83.3 us
    pallas_call x1, Pallas kernels, shards(): pl.pallas_call(place_kernel, out_shape=(jax.ShapeDtypeStruct(voxels.shape...  5.59 us
    pallas_call x1, Pallas kernels, shards(): pl.pallas_call(shear_kernel, out_shape=chunks, in_specs=[smem, hbm], out_...  5.36 us
    unnamed x10, local copies, waits for them, and re-layouts  3 us

profile of v1, /device:TPU:0, one launch (start us, length us, event | category | flops | bytes accessed | tf_op | source)
XLA Modules:
  0.0 97.9 jit_solution(7779097128203872489)
XLA Ops:
  0.6 0.0 copy-start.3
  0.6 0.6 copy-done.3
  1.3 5.4 %shear.1.xs = bf16[16,256,1024]{2,1,0:T(8,128)(2,1)S(1)} custom-call(s32[128]{0:T(128)S(1)} %copy-done.3, bf16[8,32,16384]{2,1,0:T(8,128)(2,1)} %vox_ref.1), custom_call_target="tpu_custom_call" | custom-call | tf_op jit(solution)/shard_map/shear/pallas_call | solution.py:549
  6.7 0.0 copy-start.4
  6.7 83.3 %fused.1 = (f32[32,1024]{1,0:T(8,128)}, bf16[16,256,1024]{2,1,0:T(8,128)(2,1)S(1)}, f32[32,64]{1,0:T(8,128)}, f32[33,64]{1,0:T(8,128)}) custom-call(bf16[16,256,1024]{2,1,0:T(8,128)(2,1)S(1)} %shear.1.xs, bf16[32,64]{1,0:T(8,128)(2,1)} %bitcast.2, bf16[33,64]{1,0:T(8,128)(2,1)} %second_ref.1, f32[32,1024]{1,0:T(8,128)} %cot_ref.1), custom_call_target="tpu_custom_call" | custom-call | tf_op jit(solution)/shard_map/fused/pallas_call | solution.py:558
  90.0 0.0 copy-done.4
  90.0 0.0 copy-start
  90.0 0.9 copy-done
  90.9 0.0 copy-start.1
  90.9 0.7 copy-done.1
  91.6 0.0 copy-start.2
  91.6 0.7 copy-done.2
  92.3 5.6 %place.1 = (bf16[8,32,16384]{2,1,0:T(8,128)(2,1)}, f32[32,1024]{1,0:T(8,128)}, f32[32,64]{1,0:T(8,128)}, f32[33,64]{1,0:T(8,128)}) custom-call(s32[128]{0:T(128)S(1)} %copy-done.4, bf16[16,256,1024]{2,1,0:T(8,128)(2,1)S(1)} %get-tuple-element.12.gsh_ref, f32[32,1024]{1,0:T(8,128)S(1)} %copy-done, f32[32,64]{1,0:T(8,128)S(1)} %copy-done.2, f32[33,64]{1,0:T(8,128)S(1)} %copy-done.1), custom_call_target="tpu_custom_call" | custom-call | tf_op jit(solution)/shard_map/place/pallas_call | solution.py:598
Async XLA Ops:
  0.6 0.7 copy-start.3
  6.7 83.3 %copy-start.4 = (s32[128]{0:T(128)S(1)}, s32[128]{0:T(128)}, u32[]{:S(2)}) copy-start(s32[128]{0:T(128)} %off_ref.3) | copy-start | bytes 1540
  90.0 0.9 copy-start
  90.9 0.7 copy-start.1
  91.6 0.7 copy-start.2

commit v2 on v1

--- a/solution.py
+++ b/solution.py
@@ -9,10 +9,11 @@
 
 TILE = 128
 PACK = 4
-FSUB = 256
+FSUB = 1024
 BSUB = 256
 GSUB = 512
-LIMIT = 191 * 2**18
+CSUB = 512
+LIMIT = 190 * 2**18
 BF = jnp.bfloat16
 F32 = jnp.float32
 NT = (((1,), (1,)), ((), ()))
@@ -151,6 +152,7 @@
     back,
     land,
     held,
+    raw_ref,
     give,
     got,
     mine,
@@ -285,6 +287,8 @@
             settle()
 
     fsub = min(FSUB, width)
+    csub = min(CSUB, width)
+    stack = picks((chans, planes * chans), chans, 1)
 
     def forward(i, carry):
         c = turn(i, n)
@@ -306,31 +310,37 @@
             here = pl.ds(b * fsub, fsub)
             raw_d = None
             for h in range(halves):
-                x = xs[c, pl.ds(h * kin, kin), here]
-                half = dot(w1[...], x)
+                mid = pl.ds(h * kmid, kmid)
+                half = dot(w1[...], xs[c, pl.ds(h * kin, kin), here]).astype(BF)
                 t = jnp.tanh(half)
                 up = 1.0 + t
                 hidden = half * up
-                slope[c, pl.ds(h * kmid, kmid), here] = (up + hidden * (1.0 - t)).astype(BF)
-                hidden = hidden.astype(BF)
-                hids[c, pl.ds(h * kmid, kmid), here] = hidden
+                slope[c, mid, here] = up + hidden * (1.0 - t)
+                hids[c, mid, here] = hidden
                 out = dot(w2[h], hidden)
-                srad[c, pl.ds(h * wide, wide), here] = jnp.tanh(out[:wide]).astype(BF)
+                srad[c, pl.ds(h * wide, wide), here] = jnp.tanh(out[:wide].astype(BF))
                 d = out[wide:]
                 raw_d = d if raw_d is None else raw_d + d
-            dens = softplus(raw_d) * dscale
-            upto, passing, before = absorb(dens)
-            weight = before * (1.0 - passing)
-            wgt[c, :, here] = weight
-            bpass[c, :, here] = before * passing
-            dsig[c, :, here] = dscale * (0.5 * jnp.tanh(0.5 * raw_d) + 0.5)
-            weight = 0.5 * weight
-            colour = jnp.sum(weight, axis=0, keepdims=True)
+            raw_ref[:, here] = raw_d
+        raw_d = raw_ref[...]
+        dens = softplus(raw_d) * dscale
+        upto, passing, before = absorb(dens)
+        weight = before * (1.0 - passing)
+        wgt[c] = weight
+        bpass[c] = before * passing
+        dsig[c] = dscale * (0.5 * jnp.tanh(0.5 * raw_d) + 0.5)
+        weight = 0.5 * weight
+        tsend[c] = jnp.exp(-upto[planes - 1 : planes])
+        plain = jnp.sum(weight, axis=0, keepdims=True)
+        for b in range(width // csub):
+            at = slice(b * csub, (b + 1) * csub)
+            here = pl.ds(b * csub, csub)
+            shares = []
             for p in range(planes):
-                s = srad[c, pl.ds(p * chans, chans), here].astype(F32)
-                colour = colour + weight[p : p + 1] * s
+                w = jnp.broadcast_to(weight[p : p + 1, at], (chans, csub)).astype(BF)
+                shares.append(w * srad[c, pl.ds(p * chans, chans), here])
+            colour = plain[:, at] + dot(stack, jnp.concatenate(shares, 0))
             csend[c, :, here] = colour.astype(BF)
-            tsend[c, :, here] = jnp.exp(-upto[planes - 1 : planes])
         return carry
 
     lax.fori_loop(0, n, forward, 0)
@@ -357,27 +367,33 @@
         def _():
             reply_here(c).wait_recv()
 
-        for b in range(width // bsub):
-            here = pl.ds(b * bsub, bsub)
+        for b in range(width // csub):
+            here = pl.ds(b * csub, csub)
             cot = cots[c, :, here]
             prod = jnp.concatenate(
                 [cot * srad[c, pl.ds(p * chans, chans), here] for p in range(planes)], 0
             )
-            score = 0.5 * (jnp.sum(cot.astype(F32), axis=0, keepdims=True) + dot(ones, prod))
-            enter = land[c, 0:1, here]
-            rest = land[c, 1:2, here]
-            weight = enter * wgt[c, :, here]
-            running = running_sum(weight * score)
-            grad_d = enter * bpass[c, :, here] * score - (rest - running)
-            grad_d = (grad_d * dsig[c, :, here]).astype(BF)
-            weight = 0.25 * weight
+            raw_ref[:, here] = dot(ones, prod)
+        score = 0.5 * (jnp.sum(cots[c].astype(F32), axis=0, keepdims=True) + raw_ref[...])
+        enter = land[c, 0:1, :]
+        rest = land[c, 1:2, :]
+        weight = enter * wgt[c]
+        running = running_sum(weight * score)
+        grad_d = enter * bpass[c] * score - (rest - running)
+        grad_d = (grad_d * dsig[c]).astype(BF)
+        weight = 0.25 * weight
+        for h in range(halves):
+            graw[h, pl.ds(wide, planes), :] = grad_d
+        for b in range(width // bsub):
+            at = slice(b * bsub, (b + 1) * bsub)
+            here = pl.ds(b * bsub, bsub)
+            cot = cots[c, :, here]
             for h in range(halves):
                 for k in range(PACK):
                     p = h * PACK + k
                     s = srad[c, pl.ds(p * chans, chans), here]
-                    w = jnp.broadcast_to(weight[p : p + 1], (chans, bsub)).astype(BF)
+                    w = jnp.broadcast_to(weight[p : p + 1, at], (chans, bsub)).astype(BF)
                     graw[h, pl.ds(k * chans, chans), here] = (w * cot) * (1.0 - s * s)
-                graw[h, pl.ds(wide, planes), here] = grad_d
                 ghid = dot(w2t[h], graw[h, :, here]).astype(BF)
                 mid = pl.ds(h * kmid, kmid)
                 slope[c, mid, here] = ghid * slope[c, mid, here]
@@ -445,6 +461,11 @@
     return copies
 
 
+def whole_tiles(x):
+    short = -x.shape[1] % TILE
+    return jnp.concatenate([x, jnp.zeros((x.shape[0], short), x.dtype)], 1) if short else x
+
+
 def fold_grads(n, a1_ref, a2_ref, feats, chans, give):
     hid = a1_ref.shape[0] // PACK
     halves, rows = a2_ref.shape[0], a2_ref.shape[1]
@@ -458,7 +479,7 @@
 
     g1 = g2 = gd = None
     for k in range(PACK):
-        one = aligned(a1_ref[pl.ds(k * hid, hid), :], k, feats)
+        one = aligned(whole_tiles(a1_ref[pl.ds(k * hid, hid), :]), k, feats)
         g1 = one if g1 is None else g1 + one
     for h in range(halves):
         tail = a2_ref[h, pl.ds(PACK * chans, rows - PACK * chans), :]
@@ -543,6 +564,7 @@
         jax.ShapeDtypeStruct((feats, hid), F32),
         jax.ShapeDtypeStruct((chans + 1, hid), F32),
     )
+    held = tuple(pltpu.VMEM(a.shape, F32) for a in small)
     part = (n, hid // n, TILE)
     dma = pltpu.SemaphoreType.DMA
     chunks = pltpu.VMEM((n, planes * feats, chunk), BF)
@@ -557,7 +579,7 @@
     )(offsets, pltpu.with_memory_space_constraint(voxels, pltpu.HBM))
     image, gsh, g1, g2 = pl.pallas_call(
         functools.partial(fused_kernel, dscale),
-        out_shape=(small[0], chunks) + small[1:],
+        out_shape=(held[0], chunks) + held[1:],
         in_specs=[vmem, vmem, vmem, vmem],
         out_specs=(vmem, vmem, vmem, vmem),
         scratch_shapes=[
@@ -582,6 +604,7 @@
             pltpu.VMEM((n, 2, chunk), F32),
             pltpu.VMEM((n, 2, chunk), F32),
             pltpu.VMEM((8, chunk), F32),
+            pltpu.VMEM((planes, chunk), F32),
             pltpu.VMEM(part, F32),
             pltpu.VMEM(part, F32),
             pltpu.VMEM(part[1:], F32),
@@ -603,7 +626,7 @@
         scratch_shapes=[dma],
         compiler_params=pltpu.CompilerParams(vmem_limit_bytes=4 * 2**20),
         name="place",
-    )(offsets, pltpu.with_memory_space_constraint(gsh, pltpu.VMEM), image, g1, g2)
+    )(offsets, *(pltpu.with_memory_space_constraint(a, pltpu.VMEM) for a in (gsh, image, g1, g2)))
     return image, gvox, g1.T, g2
 
 

time: 98.3 us -> 86.1 us (0.88)
  Pallas kernels: 94.2 us -> 84.6 us
  local copies, waits for them, and re-layouts: 3 us -> 0.66 us
    pallas_call x1, Pallas kernels: 83.3 us -> 73.6 us  [shards(): pl.pallas_call(functools.partial(fused_kernel, dscale), out_shape=(held[0...]
    unnamed x10 -> x4, local copies, waits for them, and re-layouts: 3 us -> 0.66 us
where the time goes in v2:
time: 86.1 us; the launch traced here: 85.9 us
  Pallas kernels  84.6 us (98%)
    pallas_call x1, Pallas kernels, shards(): pl.pallas_call(functools.partial(fused_kernel, dscale), out_shape=(held[0...  73.6 us
    pallas_call x1, Pallas kernels, shards(): pl.pallas_call(place_kernel, out_shape=(jax.ShapeDtypeStruct(voxels.shape...  5.6 us
    pallas_call x1, Pallas kernels, shards(): pl.pallas_call(shear_kernel, out_shape=chunks, in_specs=[smem, hbm], out_...  5.44 us

profile of v2, /device:TPU:0, one launch (start us, length us, event | category | flops | bytes accessed | tf_op | source)
XLA Modules:
  0.0 85.9 jit_solution(2883971802378513703)
XLA Ops:
  0.6 0.0 copy-start
  0.6 0.6 copy-done
  1.3 5.4 %shear.1.xs = bf16[16,256,1024]{2,1,0:T(8,128)(2,1)S(1)} custom-call(s32[128]{0:T(128)S(1)} %copy-done, bf16[8,32,16384]{2,1,0:T(8,128)(2,1)} %vox_ref.1), custom_call_target="tpu_custom_call" | custom-call | tf_op jit(solution)/shard_map/shear/pallas_call | solution.py:571
  6.7 0.0 copy-start.1
  6.7 73.6 %fused.1 = (f32[32,1024]{1,0:T(8,128)S(1)}, bf16[16,256,1024]{2,1,0:T(8,128)(2,1)S(1)}, f32[32,64]{1,0:T(8,128)S(1)}, f32[33,64]{1,0:T(8,128)S(1)}) custom-call(bf16[16,256,1024]{2,1,0:T(8,128)(2,1)S(1)} %shear.1.xs, bf16[32,64]{1,0:T(8,128)(2,1)} %bitcast.2, bf16[33,64]{1,0:T(8,128)(2,1)} %second_ref.1, f32[32,1024]{1,0:T(8,128)} %cot_ref.1), custom_call_target="tpu_custom_call" | custom-call | tf_op jit(solution)/shard_map/fused/pallas_call | solution.py:580
  80.3 0.0 copy-done.1
  80.3 5.6 %place.1 = (bf16[8,32,16384]{2,1,0:T(8,128)(2,1)}, f32[32,1024]{1,0:T(8,128)}, f32[32,64]{1,0:T(8,128)}, f32[33,64]{1,0:T(8,128)}) custom-call(s32[128]{0:T(128)S(1)} %copy-done.1, bf16[16,256,1024]{2,1,0:T(8,128)(2,1)S(1)} %get-tuple-element.12.gsh_ref, f32[32,1024]{1,0:T(8,128)S(1)} %get-tuple-element.13.image_in, f32[32,64]{1,0:T(8,128)S(1)} %get-tuple-element.14.g1_in, ...), custom_call_target="tpu_custom_call" | custom-call | tf_op jit(solution)/shard_map/place/pallas_call | solution.py:621
Async XLA Ops:
  0.6 0.7 copy-start
  6.7 73.6 %copy-start.1 = (s32[128]{0:T(128)S(1)}, s32[128]{0:T(128)}, u32[]{:S(2)}) copy-start(s32[128]{0:T(128)} %off_ref.3) | copy-start | bytes 1540

commit v3 on v2

--- a/solution.py
+++ b/solution.py
@@ -177,7 +177,6 @@
     feats = xs.shape[1] // planes
     kin, kmid = w1.shape[1], w1.shape[0]
     wide = rows - planes
-    lag = n // 2
     me = lax.axis_index("depth")
     chip, core = me // 2, me % 2
     partner = me + 1 - 2 * core
@@ -221,70 +220,94 @@
     def relay_copy(c):
         return remote(cots.at[c], cots.at[c], sem_r.at[c], rem_k.at[c], partner)
 
+    def relays(c):
+        return jnp.logical_and(c % 2 == core, c != me)
+
+    def give_cot(c):
+        @pl.when(c == me)
+        def _():
+            for s in range(n // 2):
+                cot_copy(s).start()
+
+    def pass_cot(c):
+        @pl.when(relays(c))
+        def _():
+            relay_copy(c).wait_recv()
+            relay_copy(c).start()
+
+    def weigh(c):
+        @pl.when(c % 2 != core)
+        def _():
+            relay_copy(c).wait_recv()
+
+        worth = cots[c].astype(F32) * csend[c].astype(F32)
+        tsend[c, 1:2, :] = jnp.sum(worth, axis=0, keepdims=True)
+
     def hand_on(c):
         @pl.when(c != me)
         def _():
+            through_copy(c).start()
+
+        @pl.when(c == me)
+        def _():
+            trecv[me] = tsend[me]
+
+    def give_colour(c):
+        @pl.when(c != me)
+        def _():
             colour_copy(c).start()
-            through_copy(c).start()
-
+
+    def settle(c):
         @pl.when(c == me)
         def _():
-            crecv[me] = csend[me]
-            trecv[me] = tsend[me]
-
-    def relays(c):
-        return jnp.logical_and(c % 2 == core, c != me)
-
-    def settle():
-        def arrived(d):
-            @pl.when(d != me)
+            def arrived(d):
+                @pl.when(d != me)
+                def _():
+                    through_here(d).wait_recv()
+
+            each(n, arrived)
+            row = lax.broadcasted_iota(jnp.int32, held.shape, 0)
+            held[...] = (row == 0).astype(F32)
+
+            def fold(d):
+                enter = held[0:1, :]
+                prior = held[1:2, :]
+                back[d, 0:1, :] = enter
+                back[d, 1:2, :] = prior
+                held[2:4, :] = trecv[d]
+                held[1:2, :] = prior + enter * held[3:4, :]
+                held[0:1, :] = enter * held[2:3, :]
+
+            each(n, fold)
+            total = held[1:2, :]
+
+            def turn_round(d):
+                back[d, 1:2, :] = total - back[d, 1:2, :]
+
+            each(n, turn_round)
+
+            def answer(d):
+                @pl.when(d != me)
+                def _():
+                    reply_copy(d).start()
+
+            each(n, answer)
+            land[me] = back[me]
+
+    duties = (
+        (n // 2 - 2, pass_cot),
+        (n // 2 + 1, weigh),
+        (n // 2 + 2, hand_on),
+        (n - 4, give_colour),
+        (n - 3, settle),
+    )
+
+    def serve(step, lags):
+        for lag, duty in lags:
+
+            @pl.when(jnp.logical_and(step >= lag, step < lag + n))
             def _():
-                colour_here(d).wait_recv()
-                through_here(d).wait_recv()
-
-        each(n, arrived)
-        cot = cot_ref[...]
-
-        row = lax.broadcasted_iota(jnp.int32, held.shape, 0)
-        held[...] = (row == 0).astype(F32)
-        image_ref[...] = jnp.zeros_like(image_ref)
-
-        def fold(d):
-            enter = held[0:1, :]
-            prior = held[1:2, :]
-            colour = crecv[d].astype(F32)
-            back[d, 0:1, :] = enter
-            back[d, 1:2, :] = prior
-            held[2:3, :] = trecv[d]
-            image_ref[...] += enter * colour
-            held[1:2, :] = prior + enter * jnp.sum(cot * colour, axis=0, keepdims=True)
-            held[0:1, :] = enter * held[2:3, :]
-
-        each(n, fold)
-        total = held[1:2, :]
-
-        def turn_round(d):
-            back[d, 1:2, :] = total - back[d, 1:2, :]
-
-        each(n, turn_round)
-
-        def answer(d):
-            @pl.when(d != me)
-            def _():
-                reply_copy(d).start()
-
-        each(n, answer)
-        land[me] = back[me]
-
-    def later(c):
-        @pl.when(relays(c))
-        def _():
-            relay_copy(c).wait_recv()
-            relay_copy(c).start()
-
-        @pl.when(c == me)
-        def _():
-            settle()
+                duty(turn(step - lag, n))
 
     fsub = min(FSUB, width)
     csub = min(CSUB, width)
@@ -293,18 +316,12 @@
     def forward(i, carry):
         c = turn(i, n)
 
-        @pl.when(i > 0)
-        def _():
-            hand_on(turn(i - 1, n))
-
-        @pl.when(c == me)
-        def _():
-            for s in range(n // 2):
-                cot_copy(s).start()
-
-        @pl.when(i >= lag)
-        def _():
-            later(turn(i - lag, n))
+        @pl.when(i < n // 2)
+        def _():
+            give_cot(turn(2 * i, n))
+            give_cot(turn(2 * i + 1, n))
+
+        serve(i, duties)
 
         for b in range(width // fsub):
             here = pl.ds(b * fsub, fsub)
@@ -330,7 +347,7 @@
         bpass[c] = before * passing
         dsig[c] = dscale * (0.5 * jnp.tanh(0.5 * raw_d) + 0.5)
         weight = 0.5 * weight
-        tsend[c] = jnp.exp(-upto[planes - 1 : planes])
+        tsend[c, 0:1, :] = jnp.exp(-upto[planes - 1 : planes])
         plain = jnp.sum(weight, axis=0, keepdims=True)
         for b in range(width // csub):
             at = slice(b * csub, (b + 1) * csub)
@@ -351,17 +368,7 @@
     def backward(i, carry):
         c = turn(i, n)
 
-        @pl.when(i == 0)
-        def _():
-            hand_on(turn(n - 1, n))
-
-        @pl.when(i < n - lag)
-        def _():
-            later(turn(i + lag, n))
-
-        @pl.when(c % 2 != core)
-        def _():
-            relay_copy(c).wait_recv()
+        serve(i + n, duties)
 
         @pl.when(c != me)
         def _():
@@ -428,6 +435,15 @@
     copies = swap(n, me, lambda to: mine, full, s2, r2)
     full[me] = mine[...]
     lax.fori_loop(n // 2, n, voxel_grads, 0)
+    image_ref[...] = back[me, 0:1, :] * csend[me].astype(F32)
+
+    def add_colour(d):
+        @pl.when(d != me)
+        def _():
+            colour_here(d).wait_recv()
+            image_ref[...] += back[d, 0:1, :] * crecv[d].astype(F32)
+
+    each(n, add_colour)
     for copy in copies:
         copy.wait()
     both = jnp.concatenate([full[d] for d in range(n)], 0)
@@ -599,8 +615,8 @@
             pltpu.VMEM((n, chans, chunk), BF),
             pltpu.VMEM((n, chans, chunk), BF),
             pltpu.VMEM((n, chans, chunk), BF),
-            pltpu.VMEM((n, 1, chunk), F32),
-            pltpu.VMEM((n, 1, chunk), F32),
+            pltpu.VMEM((n, 2, chunk), F32),
+            pltpu.VMEM((n, 2, chunk), F32),
             pltpu.VMEM((n, 2, chunk), F32),
             pltpu.VMEM((n, 2, chunk), F32),
             pltpu.VMEM((8, chunk), F32),

time: 86.1 us -> 81.8 us (0.950)
  Pallas kernels: 84.6 us -> 80.2 us
    pallas_call x1, Pallas kernels: 73.6 us -> 69.2 us  [shards(): pl.pallas_call(functools.partial(fused_kernel, dscale), out_shape=(held[0...]
where the time goes in v3:
time: 81.8 us; the launch traced here: 81.5 us
  Pallas kernels  80.2 us (98%)
    pallas_call x1, Pallas kernels, shards(): pl.pallas_call(functools.partial(fused_kernel, dscale), out_shape=(held[0...  69.2 us
    pallas_call x1, Pallas kernels, shards(): pl.pallas_call(place_kernel, out_shape=(jax.ShapeDtypeStruct(voxels.shape...  5.6 us
    pallas_call x1, Pallas kernels, shards(): pl.pallas_call(shear_kernel, out_shape=chunks, in_specs=[smem, hbm], out_...  5.37 us

profile of v3, /device:TPU:0, one launch (start us, length us, event | category | flops | bytes accessed | tf_op | source)
XLA Modules:
  0.0 81.5 jit_solution(10347671009871958275)
XLA Ops:
  0.6 0.0 copy-start
  0.6 0.6 copy-done
  1.3 5.4 %shear.1.xs = bf16[16,256,1024]{2,1,0:T(8,128)(2,1)S(1)} custom-call(s32[128]{0:T(128)S(1)} %copy-done, bf16[8,32,16384]{2,1,0:T(8,128)(2,1)} %vox_ref.1), custom_call_target="tpu_custom_call" | custom-call | tf_op jit(solution)/shard_map/shear/pallas_call | solution.py:587
  6.7 0.0 copy-start.1
  6.7 69.2 %fused.1 = (f32[32,1024]{1,0:T(8,128)S(1)}, bf16[16,256,1024]{2,1,0:T(8,128)(2,1)S(1)}, f32[32,64]{1,0:T(8,128)S(1)}, f32[33,64]{1,0:T(8,128)S(1)}) custom-call(bf16[16,256,1024]{2,1,0:T(8,128)(2,1)S(1)} %shear.1.xs, bf16[32,64]{1,0:T(8,128)(2,1)} %bitcast.2, bf16[33,64]{1,0:T(8,128)(2,1)} %second_ref.1, f32[32,1024]{1,0:T(8,128)} %cot_ref.1), custom_call_target="tpu_custom_call" | custom-call | tf_op jit(solution)/shard_map/fused/pallas_call | solution.py:596
  75.9 0.0 copy-done.1
  75.9 5.6 %place.1 = (bf16[8,32,16384]{2,1,0:T(8,128)(2,1)}, f32[32,1024]{1,0:T(8,128)}, f32[32,64]{1,0:T(8,128)}, f32[33,64]{1,0:T(8,128)}) custom-call(s32[128]{0:T(128)S(1)} %copy-done.1, bf16[16,256,1024]{2,1,0:T(8,128)(2,1)S(1)} %get-tuple-element.12.gsh_ref, f32[32,1024]{1,0:T(8,128)S(1)} %get-tuple-element.13.image_in, f32[32,64]{1,0:T(8,128)S(1)} %get-tuple-element.14.g1_in, ...), custom_call_target="tpu_custom_call" | custom-call | tf_op jit(solution)/shard_map/place/pallas_call | solution.py:637
Async XLA Ops:
  0.6 0.7 copy-start
  6.7 69.3 %copy-start.1 = (s32[128]{0:T(128)S(1)}, s32[128]{0:T(128)}, u32[]{:S(2)}) copy-start(s32[128]{0:T(128)} %off_ref.3) | copy-start | bytes 1540
